TPU v7x, 512 devices: a whole 4x4x16 slice. The times are simulated.
512 devices in a mesh: dom: 16 (over z), feat: 32 (over x, y, core).
Axes of the slice: x: 4, y: 4, z: 16, core: 2. Of those that a mesh axis runs over, the one named last changes fastest.
Arguments:
- node_feats: bfloat16 [1024, 65536], P('feat', 'dom'), may hold values from -6 to 6
- out_cotangent: bfloat16 [1024, 65536], P('feat', 'dom'), may hold values from -6 to 6
- weight_self: bfloat16 [1024, 1024], P('feat'), may hold values from -0.1875 to 0.1875
- weight_neigh: bfloat16 [1024, 1024], P('feat'), may hold values from -1.5 to 1.5
- out_bias: float32 [1024], P('feat'), may hold values from -3 to 3
- send_blocks: int32 [16, 16, 2], P('dom'), may hold values from 0 to 31
- tile_rows: int32 [16, 64], P('dom'), may hold values from 0 to 31
- tile_cols: int32 [16, 64], P('dom'), may hold values from 0 to 63
- tile_count: int32 [16], P('dom'), may hold values from 1 to 64, as said below
- tile_values: bfloat16 [16, 64, 128, 128], P('dom'), may hold values from 0 to 1
Outputs:
- layer_out: bfloat16 [1024, 65536], P('feat', 'dom')
- feats_grad: bfloat16 [1024, 65536], P('feat', 'dom')
- grad_self: float32 [1024, 1024], P('feat')
- grad_neigh: float32 [1024, 1024], P('feat')
- grad_bias: float32 [1024], P('feat')
Inputs may be any that keep to these rules, and one draw needn't show every extreme that they name: Slots t >= tile_count[p] of tile_rows, tile_cols and tile_values are not part of the graph; some partition uses all 64 slots.
All inputs are finite; a program needn't handle non-finite values.
Results may differ from a plain program's by a relative error of at most 0.0075.
Values may be sent and summed in bfloat16 or wider, within the bound.
No kernel may reach another device: no remote copies, remote signals or barrier semaphores. Data moves between devices by JAX's collectives and lax.ppermute only.
A program may use at most 64 MiB of HBM per device.

v0:
```python
import jax
import jax.numpy as jnp
from jax import lax
from jax.sharding import PartitionSpec as P

BLK = 128
NBLK = 32
CAP = 2
TMAX = 64
ROWS = 4096


def gelu_tanh(values):
    return jax.nn.gelu(values, approximate=True)


def left_product(weights, data):
    return lax.dot_general(
        weights, data, (((0,), (0,)), ((), ())), preferred_element_type=jnp.float32
    )


def per_device(
    node_feats,
    out_cotangent,
    weight_self,
    weight_neigh,
    out_bias,
    send_blocks,
    tile_rows,
    tile_cols,
    tile_count,
    tile_values,
):
    highest = lax.Precision.HIGHEST
    local_width = node_feats.shape[0]
    num_parts = lax.axis_size("dom")
    ext_blocks = NBLK + num_parts * CAP
    my_sends = send_blocks[0].reshape(num_parts * CAP)
    my_rows = tile_rows[0]
    my_cols = tile_cols[0]
    my_tiles = tile_values[0]
    live = (jnp.arange(TMAX, dtype=jnp.int32) < tile_count[0]).astype(jnp.float32)
    blocks = node_feats.reshape(local_width, NBLK, BLK)
    outgoing = blocks[:, my_sends].reshape(local_width, num_parts * CAP * BLK)
    incoming = lax.all_to_all(outgoing, "dom", split_axis=1, concat_axis=1, tiled=True)
    extended = jnp.concatenate(
        [blocks, incoming.reshape(local_width, num_parts * CAP, BLK)], axis=1
    )
    rows_hot = jax.nn.one_hot(my_rows, NBLK, dtype=jnp.float32) * live[:, None]
    picked = extended[:, my_cols]
    products = jnp.einsum("ftc,trc->ftr", picked, my_tiles, preferred_element_type=jnp.float32)
    summed = jnp.einsum("ftr,tb->fbr", products, rows_hot, precision=highest)
    degree = jnp.einsum(
        "tr,tb->br", jnp.sum(my_tiles, axis=-1, dtype=jnp.float32), rows_hot, precision=highest
    )
    divisor = jnp.maximum(degree, 1.0)
    aggregate = (summed / divisor[None]).astype(jnp.bfloat16).reshape(local_width, ROWS)
    feat_rows, agg_rows = (
        lax.all_to_all(node_feats, "feat", split_axis=1, concat_axis=0, tiled=True),
        lax.all_to_all(aggregate, "feat", split_axis=1, concat_axis=0, tiled=True),
    )
    totals = left_product(lax.all_gather(weight_self, "feat", axis=0, tiled=True), feat_rows)
    out_by_rows = totals + left_product(
        lax.all_gather(weight_neigh, "feat", axis=0, tiled=True), agg_rows
    )
    pre_act = lax.all_to_all(out_by_rows, "feat", split_axis=0, concat_axis=1, tiled=True)
    pre_act = pre_act + out_bias[:, None]
    layer_out = gelu_tanh(pre_act).astype(jnp.bfloat16)
    grad_pre = jax.vjp(gelu_tanh, pre_act)[1](out_cotangent.astype(jnp.float32))[0].astype(
        jnp.bfloat16
    )
    shard_piece = lax.all_gather(grad_pre, "feat", axis=0, tiled=True)
    self_term = lax.dot_general(
        node_feats, shard_piece, (((1,), (1,)), ((), ())), preferred_element_type=jnp.float32
    )
    neigh_term = lax.dot_general(
        aggregate, shard_piece, (((1,), (1,)), ((), ())), preferred_element_type=jnp.float32
    )
    grad_w_self = self_term
    grad_w_neigh = neigh_term
    self_back = jnp.dot(weight_self, shard_piece, preferred_element_type=jnp.float32)
    neigh_back = jnp.dot(weight_neigh, shard_piece, preferred_element_type=jnp.float32)
    grad_w_self, grad_w_neigh, self_grad, neigh_back = (
        grad_w_self,
        grad_w_neigh,
        self_back,
        neigh_back,
    )
    agg_grad = neigh_back.reshape(local_width, NBLK, BLK) / divisor[None]
    bias_term = jnp.sum(grad_pre, axis=1, dtype=jnp.float32)
    grad_w_self, grad_w_neigh, bias_total = lax.psum((grad_w_self, grad_w_neigh, bias_term), "dom")
    scale = 1.0 / jnp.sqrt(jnp.float32(ROWS * num_parts))
    grad_self = grad_w_self * scale
    grad_neigh = grad_w_neigh * scale
    grad_bias = bias_total * scale
    picked_grad = agg_grad[:, my_rows]
    contrib = jnp.einsum(
        "ftr,trc->ftc", picked_grad, my_tiles.astype(jnp.float32), precision=highest
    )
    cols_hot = jax.nn.one_hot(my_cols, ext_blocks, dtype=jnp.float32) * live[:, None]
    ext_grad = jnp.einsum("ftc,tn->fnc", contrib, cols_hot, precision=highest)
    halo_grad = ext_grad[:, NBLK:].reshape(local_width, num_parts * CAP * BLK)
    returned = lax.all_to_all(halo_grad, "dom", split_axis=1, concat_axis=1, tiled=True)
    send_hot = jax.nn.one_hot(my_sends, NBLK, dtype=jnp.float32)
    gathered_back = jnp.einsum(
        "fsc,sb->fbc",
        returned.reshape(local_width, num_parts * CAP, BLK),
        send_hot,
        precision=highest,
    )
    total = self_grad.reshape(local_width, NBLK, BLK) + ext_grad[:, :NBLK] + gathered_back
    feats_grad = total.astype(jnp.bfloat16).reshape(local_width, ROWS)
    return (layer_out, feats_grad, grad_self, grad_neigh, grad_bias)


def solution(mesh):
    in_specs = (
        P("feat", "dom"),
        P("feat", "dom"),
        P("feat", None),
        P("feat", None),
        P("feat"),
        P("dom", None, None),
        P("dom", None),
        P("dom", None),
        P("dom"),
        P("dom", None, None, None),
    )
    out_specs = (P("feat", "dom"), P("feat", "dom"), P("feat", None), P("feat", None), P("feat"))
    return jax.shard_map(
        per_device, mesh=mesh, in_specs=in_specs, out_specs=out_specs, check_vma=False
    )
```

profile of v0, /device:TPU:2, one launch (start us, length us, event | category | flops | bytes accessed | tf_op | source)
XLA Modules:
  0.0 411.8 jit_solution(10953175642827898887)
XLA Ops:
  7.2 0.0 copy-start
  7.2 0.0 all-gather.4.cloned.1.call-start
  7.2 0.7 all-gather.4.cloned.1.call-update
  7.9 0.0 all-gather.6.cloned.1.call-start
  8.0 0.7 all-gather.6.cloned.1.call-update
  8.7 0.8 copy.39
  9.4 0.1 reshape_squeeze.3
  9.6 0.7 copy_bitcast_fusion.1
  10.3 1.5 gather_fusion
  11.9 0.0 copy-start.9
  11.9 0.1 copy.41
  12.0 0.1 all_to_all.56
  12.1 0.8 copy.42
  12.9 15.2 %all-to-all-start.1 = ((bf16[32,16,256]{2,0,1:T(8,128)(2,1)}), bf16[32,16,256]{2,0,1:T(8,128)(2,1)S(1)}, u32[]{:S(2)}, u32[]{:S(2)}) async-start(bf16[32,16,256]{2,0,1:T(8,128)(2,1)} %copy.42), calls=%async_computation.1 | async-start | bytes 524288 | tf_op jit(solution)/shard_map/all_to_all | solution.py:46
  28.8 0.6 convert_reduce_fusion
  29.4 0.1 convolution_maximum_fusion
  29.6 16.9 %all-to-all-done.1 = bf16[32,16,256]{2,0,1:T(8,128)(2,1)S(1)} async-done(((bf16[32,16,256]{2,0,1:T(8,128)(2,1)}), bf16[32,16,256]{2,0,1:T(8,128)(2,1)S(1)}, u32[]{:S(2)}, u32[]{:S(2)}) %all-to-all-start.1) | async-done | bytes 262176 | tf_op jit(solution)/shard_map/all_to_all | solution.py:46
  46.5 7.7 %all-to-all-start = ((bf16[32,32,128]{2,0,1:T(8,128)(2,1)}), bf16[32,32,128]{2,0,1:T(8,128)(2,1)}, u32[]{:S(2)}, u32[]{:S(2)}) async-start(bf16[32,32,128]{2,0,1:T(8,128)(2,1)} %copy_bitcast_fusion.1), calls=%async_computation | async-start | bytes 524288 | tf_op jit(solution)/shard_map/all_to_all | solution.py:60
  54.1 0.2 copy.43
  54.3 0.1 reshape.146
  54.4 0.1 copy.45
  54.5 1.0 pad_maximum_fusion
  55.5 0.7 gather_fusion.1
  56.2 1.2 fusion.4
  57.4 1.2 fusion.12
  58.6 0.7 copy-done.3
  59.3 0.8 copy.47
  60.1 1.8 all-to-all-done
  61.9 5.6 %all-to-all-start.2 = ((bf16[32,32,128]{2,0,1:T(8,128)(2,1)}), bf16[32,32,128]{2,0,1:T(8,128)(2,1)S(1)}, u32[]{:S(2)}, u32[]{:S(2)}) async-start(bf16[32,32,128]{2,0,1:T(8,128)(2,1)} %copy.47), calls=%async_computation.2 | async-start | bytes 524288 | tf_op jit(solution)/shard_map/all_to_all | solution.py:61
  67.5 0.0 all-gather.8.cloned.1.call-start
  67.6 7.1 %all-gather.4.cloned.1.call-done = bf16[1024,1024]{1,0:T(8,128)(2,1)} async-done(((bf16[32,1024]{1,0:T(8,128)(2,1)}), bf16[1024,1024]{1,0:T(8,128)(2,1)}) %all-gather.4.cloned.1.call-update) | async-done | bytes 2097168 | tf_op jit(solution)/shard_map/all_gather | solution.py:63
  74.7 2.3 fusion.54
  77.1 60.3 %all-gather.6.cloned.1.call-done = bf16[1024,1024]{1,0:T(8,128)(2,1)} async-done(((bf16[32,1024]{1,0:T(8,128)(2,1)}), bf16[1024,1024]{1,0:T(8,128)(2,1)}) %all-gather.6.cloned.1.call-update) | async-done | bytes 2097168 | tf_op jit(solution)/shard_map/all_gather | solution.py:65
  137.4 2.6 fusion.10
  140.0 0.0 copy-start.5
  140.0 15.6 %all_to_all.72 = f32[32,32,128]{2,1,0:T(8,128)S(1)} all-to-all(f32[32,32,128]{2,1,0:T(8,128)S(1)} %bitcast.119), channel_id=1, replica_groups=mesh['dom'=16,'feat'=32] {'feat'}, dimensions={0} | all-to-all | bytes 1048576 | tf_op jit(solution)/shard_map/all_to_all | solution.py:67
  155.6 1.4 convert_reduce_fusion.1
  157.0 0.0 all-gather.8.cloned.1.call-update
  157.0 0.0 copy-start.6
  157.0 67.5 %all-gather.8.cloned.1.call-done = bf16[1024,4096]{1,0:T(8,128)(2,1)} async-done(((bf16[32,4096]{1,0:T(8,128)(2,1)}), bf16[1024,4096]{1,0:T(8,128)(2,1)}) %all-gather.8.cloned.1.call-update) | async-done | bytes 8388624 | tf_op jit(solution)/shard_map/all_gather | solution.py:73
  224.6 5.1 %convolution_bitcast_fusion.1 = f32[4,32,8,128]{3,2,1,0:T(8,128)S(1)} fusion(bf16[32,1024]{1,0:T(8,128)(2,1)S(1)} %copy-done.5, bf16[1024,4096]{1,0:T(8,128)(2,1)} %all-gather.8.cloned.1.call-done), kind=kOutput, calls=%fused_computation.11 | convolution fusion | flops 268435456 | bytes 8978432 | tf_op jit(solution)/shard_map/dot_general | solution.py:83
  229.7 0.1 bitcast_divide_fusion
  229.7 0.6 copy-done.1
  230.4 1.5 convolution_bitcast_fusion.2
  231.9 0.1 copy.59
  232.0 1.7 gather_fusion.2
  233.7 3.0 fusion.7
  236.7 1.6 convolution_bitcast_fusion
  238.3 0.1 fusion.53
  238.4 0.1 all_to_all.65
  238.6 1.2 copy.53
  239.7 12.3 %all-to-all-start.4 = ((f32[32,16,256]{2,0,1:T(8,128)}), f32[32,16,256]{2,0,1:T(8,128)S(1)}, u32[]{:S(2)}, u32[]{:S(2)}) async-start(f32[32,16,256]{2,0,1:T(8,128)} %copy.53), calls=%async_computation.4 | async-start | bytes 1048576 | tf_op jit(solution)/shard_map/all_to_all | solution.py:104
  252.0 0.0 all-reduce.3.cloned.1.call-start
  252.1 6.7 %convolution_bitcast_fusion.5 = f32[32,1024]{1,0:T(8,128)} fusion(bf16[1024,4096]{1,0:T(8,128)(2,1)} %all-gather.8.cloned.1.call-done, bf16[32,4096]{1,0:T(8,128)(2,1)S(1)} %copy-done), kind=kOutput, calls=%fused_computation.20 | convolution fusion | flops 268435456 | bytes 8781824 | tf_op jit(solution)/shard_map/dot_general | solution.py:74
  258.7 6.6 %fusion.28 = f32[32,1024]{1,0:T(8,128)} fusion(bf16[1024,4096]{1,0:T(8,128)(2,1)} %all-gather.8.cloned.1.call-done, bf16[4,8,32,128]{3,2,1,0:T(8,128)(2,1)S(1)} %bitcast.121), kind=kOutput, calls=%fused_computation.46 | convolution fusion | flops 268435456 | bytes 8781824 | tf_op jit(solution)/shard_map/dot_general | solution.py:77
  265.4 0.0 all-reduce.3.cloned.1.call-update
  265.4 0.1 eq.74
  265.5 35.6 %psum.23 = f32[32]{0:T(128)S(1)} all-reduce(f32[32]{0:T(128)S(1)} %get-tuple-element.7), channel_id=1, replica_groups=mesh['dom'=16,'feat'=32] {'dom'}, use_global_device_ids=true, to_apply=%region_4.5 | all-reduce | flops 32 | bytes 256 | tf_op jit(solution)/shard_map/psum | solution.py:92
  301.1 0.5 broadcast_multiply_fusion.2
  301.6 100.5 %all-reduce.3.cloned.1.call-done = (f32[32,1024]{1,0:T(8,128)}, f32[32,1024]{1,0:T(8,128)}) async-done(((f32[32,1024]{1,0:T(8,128)}, f32[32,1024]{1,0:T(8,128)}), (f32[32,1024]{1,0:T(8,128)}, f32[32,1024]{1,0:T(8,128)})) %all-reduce.3.cloned.1.call-update) | async-done | bytes 262160 | tf_op jit(solution)/shard_map/psum | solution.py:92
  402.1 1.7 broadcast_multiply_fusion
  403.8 0.3 copy.54
  404.1 0.4 fusion.13
  404.5 0.8 copy.85
  (26 shorter events, 0.1 us)
Async XLA Ops:
  7.2 2.4 copy-start
  7.2 21.6 %copy-start.10 = (s32[1,64]{1,0:T(1,128)S(1)}, s32[1,64]{1,0:T(1,128)}, u32[]{:S(2)}) copy-start(s32[1,64]{1,0:T(1,128)} %param.17) | copy-start | bytes 772
  7.2 21.6 %copy-start.2 = (bf16[1,64,128,128]{3,2,1,0:T(8,128)(2,1)S(1)}, bf16[1,64,128,128]{3,2,1,0:T(8,128)(2,1)}, u32[]{:S(2)}) copy-start(bf16[1,64,128,128]{3,2,1,0:T(8,128)(2,1)} %param.19) | copy-start | bytes 6291460
  7.2 67.5 %all-gather.4.cloned.1.call-start = ((), (), s32[]{:S(2)}) async-start(), calls=%async_computation.5 | async-start | bytes 2162688 | tf_op jit(solution)/shard_map/all_gather | solution.py:63
  7.9 129.5 %all-gather.6.cloned.1.call-start = ((), (), s32[]{:S(2)}) async-start(), calls=%async_computation.6 | async-start | bytes 2162688 | tf_op jit(solution)/shard_map/all_gather | solution.py:65
  11.9 17.5 %copy-start.9 = (s32[1,64]{1,0:T(1,128)S(1)}, s32[1,64]{1,0:T(1,128)}, u32[]{:S(2)}) copy-start(s32[1,64]{1,0:T(1,128)} %param.16) | copy-start | bytes 772
  12.9 33.6 %all-to-all-start.1 = ((bf16[32,16,256]{2,0,1:T(8,128)(2,1)}), bf16[32,16,256]{2,0,1:T(8,128)(2,1)S(1)}, u32[]{:S(2)}, u32[]{:S(2)}) async-start(bf16[32,16,256]{2,0,1:T(8,128)(2,1)} %copy.42), calls=%async_computation.1 | async-start | bytes 524288 | tf_op jit(solution)/shard_map/all_to_all | solution.py:46
  46.5 15.4 %all-to-all-start = ((bf16[32,32,128]{2,0,1:T(8,128)(2,1)}), bf16[32,32,128]{2,0,1:T(8,128)(2,1)}, u32[]{:S(2)}, u32[]{:S(2)}) async-start(bf16[32,32,128]{2,0,1:T(8,128)(2,1)} %copy_bitcast_fusion.1), calls=%async_computation | async-start | bytes 524288 | tf_op jit(solution)/shard_map/all_to_all | solution.py:60
  58.6 0.7 copy-start.3
  61.9 15.2 %all-to-all-start.2 = ((bf16[32,32,128]{2,0,1:T(8,128)(2,1)}), bf16[32,32,128]{2,0,1:T(8,128)(2,1)S(1)}, u32[]{:S(2)}, u32[]{:S(2)}) async-start(bf16[32,32,128]{2,0,1:T(8,128)(2,1)} %copy.47), calls=%async_computation.2 | async-start | bytes 524288 | tf_op jit(solution)/shard_map/all_to_all | solution.py:61
  67.5 157.1 %all-gather.8.cloned.1.call-start = ((), (), s32[]{:S(2)}) async-start(), calls=%async_computation.7 | async-start | bytes 8650752 | tf_op jit(solution)/shard_map/all_gather | solution.py:73
  137.4 18.2 %copy-start.7 = (bf16[32,4096]{1,0:T(8,128)(2,1)S(1)}, bf16[32,4096]{1,0:T(8,128)(2,1)}, u32[]{:S(2)}) copy-start(bf16[32,4096]{1,0:T(8,128)(2,1)} %param.11) | copy-start | bytes 786436
  137.4 18.2 %copy-start.8 = (f32[32]{0:T(128)S(1)}, f32[32]{0:T(128)}, u32[]{:S(2)}) copy-start(f32[32]{0:T(128)} %param.14) | copy-start | bytes 388
  140.0 84.6 %copy-start.5 = (bf16[32,1024]{1,0:T(8,128)(2,1)S(1)}, bf16[32,1024]{1,0:T(8,128)(2,1)}, u32[]{:S(2)}) copy-start(bf16[32,1024]{1,0:T(8,128)(2,1)} %param.13) | copy-start | bytes 196612
  157.0 72.7 %copy-start.6 = (bf16[32,1024]{1,0:T(8,128)(2,1)S(1)}, bf16[32,1024]{1,0:T(8,128)(2,1)}, u32[]{:S(2)}) copy-start(bf16[32,1024]{1,0:T(8,128)(2,1)} %param.12) | copy-start | bytes 196612
  224.6 5.8 %copy-start.1 = (bf16[1024,4096]{1,0:T(8,128)(2,1)S(1)}, bf16[1024,4096]{1,0:T(8,128)(2,1)}, u32[]{:S(2)}) copy-start(bf16[1024,4096]{1,0:T(8,128)(2,1)} %all-gather.8.cloned.1.call-done) | copy-start | bytes 25165828
  239.7 164.0 %all-to-all-start.4 = ((f32[32,16,256]{2,0,1:T(8,128)}), f32[32,16,256]{2,0,1:T(8,128)S(1)}, u32[]{:S(2)}, u32[]{:S(2)}) async-start(f32[32,16,256]{2,0,1:T(8,128)} %copy.53), calls=%async_computation.4 | async-start | bytes 1048576 | tf_op jit(solution)/shard_map/all_to_all | solution.py:104
  252.0 6.7 %copy-start.4 = (bf16[32,32,128]{2,0,1:T(8,128)(2,1)S(1)}, bf16[32,32,128]{2,0,1:T(8,128)(2,1)}, u32[]{:S(2)}) copy-start(bf16[32,32,128]{2,0,1:T(8,128)(2,1)} %copy-done.3) | copy-start | bytes 786436
  252.0 150.0 %all-reduce.3.cloned.1.call-start = ((), (), s32[]{:S(2)}) async-start(), calls=%async_computation.8 | async-start | bytes 524288 | tf_op jit(solution)/shard_map/psum | solution.py:92
Sparse Core Ops, SparseCore 0:
  11.1 63.5 all-gather.3
  77.9 59.4 all-gather.5
  157.1 67.4 all-gather.7
  265.5 136.5 all-reduce.2
where the time goes:
time: 413 us; the launch traced here: 412 us
  waiting for transfers between devices  256 us (62%)
  blocking collectives  51.2 us (12%)
  starting transfers between devices  40.9 us (10%)
  matrix products  32.3 us (8%)
  between operations  14.8 us (4%)
  local copies, waits for them, and re-layouts  11.6 us (3%)
  other arithmetic  5.43 us (1%)
    psum x1, waiting for transfers between devices, per_device(): lax.psum((grad_w_self, grad_w_neigh, bias_term), 'dom')  100 us
    all_gather x1, waiting for transfers between devices, per_device(): shard_piece = lax.all_gather(grad_pre, 'feat', axis=0, tiled=True)  67.5 us
    all_gather x1, waiting for transfers between devices, per_device(): lax.all_gather(weight_neigh, 'feat', axis=0, tiled=True)  60.3 us
    psum x1, blocking collectives, per_device(): lax.psum((grad_w_self, grad_w_neigh, bias_term), 'dom')  35.6 us
    all_to_all x1, waiting for transfers between devices, per_device(): lax.all_to_all(outgoing, 'dom', split_axis=1, concat_axis=1, tiled=True)  16.9 us
    all_to_all x1, blocking collectives, per_device(): lax.all_to_all(out_by_rows, 'feat', split_axis=0, concat_axis=1, tiled=True)  15.6 us
    all_to_all x1, starting transfers between devices, per_device(): lax.all_to_all(outgoing, 'dom', split_axis=1, concat_axis=1, tiled=True)  15.2 us
    all_to_all x1, starting transfers between devices, per_device(): lax.all_to_all(halo_grad, 'dom', split_axis=1, concat_axis=1, tiled=True)  12.3 us
  transfers between devices with their start and end apart: 8, of which 6 were waited for; matrix products, arithmetic and copies ran while one was open for 7% of the time, Pallas kernels for 0%

commit v1 on v0

--- a/solution.py
+++ b/solution.py
@@ -62,7 +62,10 @@
     )
     totals = left_product(lax.all_gather(weight_self, "feat", axis=0, tiled=True), feat_rows)
     out_by_rows = totals + left_product(
-        lax.all_gather(weight_neigh, "feat", axis=0, tiled=True), agg_rows
+        jnp.concatenate(
+            lax.all_to_all(jnp.stack([weight_neigh] * lax.axis_size("feat")), "feat", 0, 0), axis=0
+        ),
+        agg_rows,
     )
     pre_act = lax.all_to_all(out_by_rows, "feat", split_axis=0, concat_axis=1, tiled=True)
     pre_act = pre_act + out_bias[:, None]

time: 413 us -> 382 us (0.925)
  waiting for transfers between devices: 256 us -> 183 us
  blocking collectives: 51.2 us -> 100 us
  starting transfers between devices: 40.9 us -> 34 us
    all_gather x1 -> x0, waiting for transfers between devices: 60.3 us -> none  [per_device(): lax.all_gather(weight_neigh, 'feat', axis=0, tiled=True)]
    all_to_all x0 -> x2, blocking collectives: none -> 49.9 us  [the longest x1 34.8 us: per_device(): lax.all_to_all(jnp.stack([weight_neigh] * lax.axis_size('feat')), 'feat',...]
    all_gather x1, waiting for transfers between devices: 7.15 us -> 0.01 us  [per_device(): lax.all_gather(weight_self, 'feat', axis=0, tiled=True)]
    all_gather x1, waiting for transfers between devices: 67.5 us -> 61.1 us  [per_device(): shard_piece = lax.all_gather(grad_pre, 'feat', axis=0, tiled=True)]
    all_to_all x1 -> x0, starting transfers between devices: 5.62 us -> none  [per_device(): lax.all_to_all(aggregate, 'feat', split_axis=1, concat_axis=0, tiled=True)]
  transfers between devices with their start and end apart: 8 -> 6, of which waited for: 6 -> 4; matrix products, arithmetic and copies ran while one was open for 7% -> 6% of each run, Pallas kernels for 0% -> 0%
where the time goes in v1:
time: 382 us; the launch traced here: 381 us
  waiting for transfers between devices  183 us (48%)
  blocking collectives  100 us (26%)
  starting transfers between devices  34 us (9%)
  matrix products  32.9 us (9%)
  between operations  14.7 us (4%)
  local copies, waits for them, and re-layouts  11.2 us (3%)
  other arithmetic  5.43 us (1%)
    psum x1, waiting for transfers between devices, per_device(): lax.psum((grad_w_self, grad_w_neigh, bias_term), 'dom')  100 us
    all_gather x1, waiting for transfers between devices, per_device(): shard_piece = lax.all_gather(grad_pre, 'feat', axis=0, tiled=True)  61.1 us
    psum x1, blocking collectives, per_device(): lax.psum((grad_w_self, grad_w_neigh, bias_term), 'dom')  35.6 us
    all_to_all x1, blocking collectives, per_device(): lax.all_to_all(jnp.stack([weight_neigh] * lax.axis_size('feat')), 'feat',...  34.8 us
    all_to_all x1, waiting for transfers between devices, per_device(): lax.all_to_all(outgoing, 'dom', split_axis=1, concat_axis=1, tiled=True)  16.2 us
    all_to_all x1, starting transfers between devices, per_device(): lax.all_to_all(outgoing, 'dom', split_axis=1, concat_axis=1, tiled=True)  15.2 us
    all_to_all x1, blocking collectives, per_device(): lax.all_to_all(aggregate, 'feat', split_axis=1, concat_axis=0, tiled=True)  15.1 us
    all_to_all x1, blocking collectives, per_device(): lax.all_to_all(out_by_rows, 'feat', split_axis=0, concat_axis=1, tiled=True)  14.5 us
  transfers between devices with their start and end apart: 6, of which 4 were waited for; matrix products, arithmetic and copies ran while one was open for 6% of the time, Pallas kernels for 0%

profile of v1, /device:TPU:2, one launch (start us, length us, event | category | flops | bytes accessed | tf_op | source)
XLA Modules:
  0.0 381.2 jit_solution(14127530618066815586)
XLA Ops:
  7.2 0.0 copy-start
  7.2 0.9 copy.39
  8.1 0.1 reshape_squeeze.3
  8.2 0.0 copy-done
  8.2 0.7 copy_bitcast_fusion.1
  9.0 1.5 gather_fusion
  10.5 0.0 copy-start.9
  10.5 0.1 copy.41
  10.7 0.1 all_to_all.57
  10.8 0.8 copy.42
  11.5 15.2 %all-to-all-start.1 = ((bf16[32,16,256]{2,0,1:T(8,128)(2,1)}), bf16[32,16,256]{2,0,1:T(8,128)(2,1)S(1)}, u32[]{:S(2)}, u32[]{:S(2)}) async-start(bf16[32,16,256]{2,0,1:T(8,128)(2,1)} %copy.42), calls=%async_computation.1 | async-start | bytes 524288 | tf_op jit(solution)/shard_map/all_to_all | solution.py:46
  26.7 0.0 all-gather.3.cloned.1.call-start
  26.8 0.7 all-gather.3.cloned.1.call-update
  28.2 0.6 convert_reduce_fusion
  28.8 0.1 convolution_maximum_fusion
  29.0 16.2 %all-to-all-done.1 = bf16[32,16,256]{2,0,1:T(8,128)(2,1)S(1)} async-done(((bf16[32,16,256]{2,0,1:T(8,128)(2,1)}), bf16[32,16,256]{2,0,1:T(8,128)(2,1)S(1)}, u32[]{:S(2)}, u32[]{:S(2)}) %all-to-all-start.1) | async-done | bytes 262176 | tf_op jit(solution)/shard_map/all_to_all | solution.py:46
  45.1 0.1 copy.43
  45.3 0.1 reshape.149
  45.4 0.1 copy.45
  45.5 1.0 pad_maximum_fusion
  46.5 0.7 gather_fusion.1
  47.2 1.2 fusion.6
  48.3 1.2 fusion.16
  49.6 0.1 copy.47
  49.7 0.6 copy-done.3
  50.3 15.1 %all_to_all.74 = bf16[32,32,128]{2,0,1:T(8,128)(2,1)S(1)} all-to-all(bf16[32,32,128]{2,0,1:T(8,128)(2,1)S(1)} %copy.47), channel_id=1, replica_groups=mesh['dom'=16,'feat'=32] {'feat'}, dimensions={1} | all-to-all | bytes 524288 | tf_op jit(solution)/shard_map/all_to_all | solution.py:61
  65.4 0.0 copy-done.5
  65.4 0.2 stack.2
  65.7 34.8 %all_to_all.75 = bf16[32,32,1024]{2,1,0:T(8,128)(2,1)} all-to-all(bf16[32,32,1024]{2,1,0:T(8,128)(2,1)S(1)} %stack.2), channel_id=1, replica_groups=mesh['dom'=16,'feat'=32] {'feat'}, dimensions={0} | all-to-all | bytes 4194304 | tf_op jit(solution)/shard_map/all_to_all | solution.py:66
  100.4 6.4 %all-to-all-start = ((bf16[32,32,128]{2,0,1:T(8,128)(2,1)}), bf16[32,32,128]{2,0,1:T(8,128)(2,1)S(1)}, u32[]{:S(2)}, u32[]{:S(2)}) async-start(bf16[32,32,128]{2,0,1:T(8,128)(2,1)} %copy_bitcast_fusion.1), calls=%async_computation | async-start | bytes 524288 | tf_op jit(solution)/shard_map/all_to_all | solution.py:60
  106.8 0.0 all-gather.5.cloned.1.call-start
  106.9 3.1 fusion.12
  110.0 4.5 %all-to-all-done = bf16[32,32,128]{2,0,1:T(8,128)(2,1)S(1)} async-done(((bf16[32,32,128]{2,0,1:T(8,128)(2,1)}), bf16[32,32,128]{2,0,1:T(8,128)(2,1)S(1)}, u32[]{:S(2)}, u32[]{:S(2)}) %all-to-all-start) | async-done | bytes 262176 | tf_op jit(solution)/shard_map/all_to_all | solution.py:60
  114.5 2.4 convolution_add_fusion
  116.9 14.5 %all_to_all.76 = f32[32,32,128]{2,1,0:T(8,128)S(1)} all-to-all(f32[32,32,128]{2,1,0:T(8,128)S(1)} %bitcast.117), channel_id=1, replica_groups=mesh['dom'=16,'feat'=32] {'feat'}, dimensions={0} | all-to-all | bytes 1048576 | tf_op jit(solution)/shard_map/all_to_all | solution.py:70
  131.4 1.4 convert_reduce_fusion.1
  132.8 0.0 all-gather.5.cloned.1.call-update
  132.9 0.0 copy-start.6
  132.9 61.1 %all-gather.5.cloned.1.call-done = bf16[1024,4096]{1,0:T(8,128)(2,1)} async-done(((bf16[32,4096]{1,0:T(8,128)(2,1)}), bf16[1024,4096]{1,0:T(8,128)(2,1)}) %all-gather.5.cloned.1.call-update) | async-done | bytes 8388624 | tf_op jit(solution)/shard_map/all_gather | solution.py:76
  194.0 5.1 %convolution_bitcast_fusion.1 = f32[4,32,8,128]{3,2,1,0:T(8,128)S(1)} fusion(bf16[32,1024]{1,0:T(8,128)(2,1)S(1)} %copy-done.5, bf16[1024,4096]{1,0:T(8,128)(2,1)} %all-gather.5.cloned.1.call-done), kind=kOutput, calls=%fused_computation.14 | convolution fusion | flops 268435456 | bytes 8978432 | tf_op jit(solution)/shard_map/dot_general | solution.py:86
  199.0 0.1 bitcast_divide_fusion
  199.1 0.6 copy-done.1
  199.7 1.5 convolution_bitcast_fusion.2
  201.3 0.1 copy.62
  201.4 1.7 gather_fusion.2
  203.1 3.0 fusion.9
  206.0 1.6 convolution_bitcast_fusion
  207.6 0.1 fusion.59
  207.8 0.1 all_to_all.66
  207.9 1.1 copy.55
  209.1 12.3 %all-to-all-start.5 = ((f32[32,16,256]{2,0,1:T(8,128)}), f32[32,16,256]{2,0,1:T(8,128)S(1)}, u32[]{:S(2)}, u32[]{:S(2)}) async-start(f32[32,16,256]{2,0,1:T(8,128)} %copy.55), calls=%async_computation.5 | async-start | bytes 1048576 | tf_op jit(solution)/shard_map/all_to_all | solution.py:107
  221.4 0.0 all-reduce.3.cloned.1.call-start
  221.4 6.7 %convolution_bitcast_fusion.4 = f32[32,1024]{1,0:T(8,128)} fusion(bf16[1024,4096]{1,0:T(8,128)(2,1)} %all-gather.5.cloned.1.call-done, bf16[32,4096]{1,0:T(8,128)(2,1)S(1)} %copy-done), kind=kOutput, calls=%fused_computation.22 | convolution fusion | flops 268435456 | bytes 8781824 | tf_op jit(solution)/shard_map/dot_general | solution.py:77
  228.1 6.6 %fusion.32 = f32[32,1024]{1,0:T(8,128)} fusion(bf16[1024,4096]{1,0:T(8,128)(2,1)} %all-gather.5.cloned.1.call-done, bf16[4,8,32,128]{3,2,1,0:T(8,128)(2,1)S(1)} %bitcast.119), kind=kOutput, calls=%fused_computation.48 | convolution fusion | flops 268435456 | bytes 8781824 | tf_op jit(solution)/shard_map/dot_general | solution.py:80
  234.7 0.0 all-reduce.3.cloned.1.call-update
  234.7 0.1 eq.74
  234.8 35.6 %psum.23 = f32[32]{0:T(128)S(1)} all-reduce(f32[32]{0:T(128)S(1)} %get-tuple-element.7), channel_id=1, replica_groups=mesh['dom'=16,'feat'=32] {'dom'}, use_global_device_ids=true, to_apply=%region_4.5 | all-reduce | flops 32 | bytes 256 | tf_op jit(solution)/shard_map/psum | solution.py:95
  270.5 0.5 broadcast_multiply_fusion.2
  271.0 100.4 %all-reduce.3.cloned.1.call-done = (f32[32,1024]{1,0:T(8,128)}, f32[32,1024]{1,0:T(8,128)}) async-done(((f32[32,1024]{1,0:T(8,128)}, f32[32,1024]{1,0:T(8,128)}), (f32[32,1024]{1,0:T(8,128)}, f32[32,1024]{1,0:T(8,128)})) %all-reduce.3.cloned.1.call-update) | async-done | bytes 262160 | tf_op jit(solution)/shard_map/psum | solution.py:95
  371.4 1.7 broadcast_multiply_fusion
  373.1 0.0 all-to-all-done.5
  373.1 0.3 copy.56
  373.5 0.4 fusion.17
  373.9 0.8 copy.96
  (24 shorter events, 0.1 us)
Async XLA Ops:
  7.2 1.1 copy-start
  7.2 21.0 %copy-start.10 = (s32[1,64]{1,0:T(1,128)S(1)}, s32[1,64]{1,0:T(1,128)}, u32[]{:S(2)}) copy-start(s32[1,64]{1,0:T(1,128)} %param.17) | copy-start | bytes 772
  7.2 21.0 %copy-start.2 = (bf16[1,64,128,128]{3,2,1,0:T(8,128)(2,1)S(1)}, bf16[1,64,128,128]{3,2,1,0:T(8,128)(2,1)}, u32[]{:S(2)}) copy-start(bf16[1,64,128,128]{3,2,1,0:T(8,128)(2,1)} %param.19) | copy-start | bytes 6291460
  10.5 18.3 %copy-start.9 = (s32[1,64]{1,0:T(1,128)S(1)}, s32[1,64]{1,0:T(1,128)}, u32[]{:S(2)}) copy-start(s32[1,64]{1,0:T(1,128)} %param.16) | copy-start | bytes 772
  11.5 33.6 %all-to-all-start.1 = ((bf16[32,16,256]{2,0,1:T(8,128)(2,1)}), bf16[32,16,256]{2,0,1:T(8,128)(2,1)S(1)}, u32[]{:S(2)}, u32[]{:S(2)}) async-start(bf16[32,16,256]{2,0,1:T(8,128)(2,1)} %copy.42), calls=%async_computation.1 | async-start | bytes 524288 | tf_op jit(solution)/shard_map/all_to_all | solution.py:46
  26.7 87.8 %all-gather.3.cloned.1.call-start = ((), (), s32[]{:S(2)}) async-start(), calls=%async_computation.6 | async-start | bytes 2162688 | tf_op jit(solution)/shard_map/all_gather | solution.py:63
  48.3 17.1 %copy-start.5 = (bf16[32,1024]{1,0:T(8,128)(2,1)S(1)}, bf16[32,1024]{1,0:T(8,128)(2,1)}, u32[]{:S(2)}) copy-start(bf16[32,1024]{1,0:T(8,128)(2,1)} %param.13) | copy-start | bytes 196612
  49.6 0.7 copy-start.3
  100.4 14.1 %all-to-all-start = ((bf16[32,32,128]{2,0,1:T(8,128)(2,1)}), bf16[32,32,128]{2,0,1:T(8,128)(2,1)S(1)}, u32[]{:S(2)}, u32[]{:S(2)}) async-start(bf16[32,32,128]{2,0,1:T(8,128)(2,1)} %copy_bitcast_fusion.1), calls=%async_computation | async-start | bytes 524288 | tf_op jit(solution)/shard_map/all_to_all | solution.py:60
  106.8 87.1 %all-gather.5.cloned.1.call-start = ((), (), s32[]{:S(2)}) async-start(), calls=%async_computation.7 | async-start | bytes 8650752 | tf_op jit(solution)/shard_map/all_gather | solution.py:76
  114.5 16.9 %copy-start.7 = (bf16[32,4096]{1,0:T(8,128)(2,1)S(1)}, bf16[32,4096]{1,0:T(8,128)(2,1)}, u32[]{:S(2)}) copy-start(bf16[32,4096]{1,0:T(8,128)(2,1)} %param.11) | copy-start | bytes 786436
  114.5 16.9 %copy-start.8 = (f32[32]{0:T(128)S(1)}, f32[32]{0:T(128)}, u32[]{:S(2)}) copy-start(f32[32]{0:T(128)} %param.14) | copy-start | bytes 388
  132.9 66.2 %copy-start.6 = (bf16[32,1024]{1,0:T(8,128)(2,1)S(1)}, bf16[32,1024]{1,0:T(8,128)(2,1)}, u32[]{:S(2)}) copy-start(bf16[32,1024]{1,0:T(8,128)(2,1)} %param.12) | copy-start | bytes 196612
  194.0 5.8 %copy-start.1 = (bf16[1024,4096]{1,0:T(8,128)(2,1)S(1)}, bf16[1024,4096]{1,0:T(8,128)(2,1)}, u32[]{:S(2)}) copy-start(bf16[1024,4096]{1,0:T(8,128)(2,1)} %all-gather.5.cloned.1.call-done) | copy-start | bytes 25165828
  209.1 164.0 %all-to-all-start.5 = ((f32[32,16,256]{2,0,1:T(8,128)}), f32[32,16,256]{2,0,1:T(8,128)S(1)}, u32[]{:S(2)}, u32[]{:S(2)}) async-start(f32[32,16,256]{2,0,1:T(8,128)} %copy.55), calls=%async_computation.5 | async-start | bytes 1048576 | tf_op jit(solution)/shard_map/all_to_all | solution.py:107
  221.4 6.7 %copy-start.4 = (bf16[32,32,128]{2,0,1:T(8,128)(2,1)S(1)}, bf16[32,32,128]{2,0,1:T(8,128)(2,1)}, u32[]{:S(2)}) copy-start(bf16[32,32,128]{2,0,1:T(8,128)(2,1)} %copy-done.3) | copy-start | bytes 786436
  221.4 150.0 %all-reduce.3.cloned.1.call-start = ((), (), s32[]{:S(2)}) async-start(), calls=%async_computation.8 | async-start | bytes 524288 | tf_op jit(solution)/shard_map/psum | solution.py:95
Sparse Core Ops, SparseCore 0:
  30.7 70.0 all-gather.2
  133.0 60.9 all-gather.4
  234.9 136.5 all-reduce.2
